TPU v7x, 128 devices: a whole 4x4x4 slice. The times are simulated.
128 devices in a mesh: outer: 8 (over z, core), inner: 16 (over y, x).
Axes of the slice: x: 4, y: 4, z: 4, core: 2. Of those that a mesh axis runs over, the one named last changes fastest.
Arguments:
- queries: bfloat16 [131072, 2048], P(('outer', 'inner')), may hold values from -6 to 6
- keys: bfloat16 [131072, 2048], P(('outer', 'inner')), may hold values from -6 to 6
- values: bfloat16 [131072, 2048], P(('outer', 'inner')), may hold values from -6 to 6
- level_weights: float32 [12, 32], replicated, may hold values from 0.1 to 1
- out_weight: bfloat16 [2048, 2048], replicated, may hold values from -0.125 to 0.125
Outputs:
- mixed_out: bfloat16 [131072, 2048], P(('outer', 'inner'))
All inputs are finite; a program needn't handle non-finite values.
Results may differ from a plain program's by a relative error of at most 0.0071.
Values sent between devices are 32-bit elements; how exact they have to be, the bound alone decides.
No kernel may reach another device: no remote copies, remote signals or barrier semaphores. Data moves between devices by JAX's collectives and lax.ppermute only.
A program may use at most 256 MiB of HBM per device.

v0:
```python
import functools
import math

import jax
import jax.numpy as jnp
from jax import lax
from jax.experimental import pallas as pl
from jax.experimental.pallas import tpu as pltpu
from jax.sharding import PartitionSpec as P


SPAN = 64
LANES = 128
WIDE = 256
TOTALS_WIDE = 512
LAST = 2
INSIDE_MIB = 32
FINISH_MIB = 40
EPS = 1e-06


def in_hbm(array):
    return pltpu.with_memory_space_constraint(array, pltpu.HBM)


def mib(count):
    return count * 1024 * 1024


def same_head(size, kind):
    row = lax.broadcasted_iota(jnp.int32, (size, size), 0) // SPAN
    col = lax.broadcasted_iota(jnp.int32, (size, size), 1) // SPAN
    return jnp.where(row == col, 1.0, 0.0).astype(kind)


def inverse_norm(block):
    total = jnp.dot(
        block * block, same_head(block.shape[1], block.dtype), preferred_element_type=jnp.float32
    )
    return lax.rsqrt(total + EPS)


def scaled(block, factor):
    return (block.astype(jnp.float32) * factor).astype(jnp.bfloat16)


def pair_state(turned, values):
    both = jnp.dot(turned, values, preferred_element_type=jnp.float32)
    lane = lax.broadcasted_iota(jnp.int32, (SPAN, LANES), 1)
    return jnp.where(lane < SPAN, both[:SPAN], both[SPAN:])


def by_head(block, low):
    zero = jnp.zeros_like(block)
    return jnp.concatenate([jnp.where(low, block, zero), jnp.where(low, zero, block)], axis=0)


def totals_kernel(where_ref, k_hbm, v_hbm, kt_hbm, *refs):
    outs = refs[:4]
    k_buf, v_buf, kt_buf, held, k_sem, v_sem, kt_sem = refs[4:]
    groups = k_buf.shape[0]
    each = TOTALS_WIDE // WIDE

    def load(hbm, buf, sem, group):
        return pltpu.make_async_copy(
            hbm.at[:, group * WIDE : (group + 1) * WIDE], buf.at[group], sem.at[group]
        )

    keys = [load(k_hbm, k_buf, k_sem, group) for group in range(groups)]
    values = [load(v_hbm, v_buf, v_sem, group) for group in range(groups)]
    stores = [
        pltpu.make_async_copy(
            kt_buf.at[group], kt_hbm.at[group * WIDE : (group + 1) * WIDE, :], kt_sem.at[group]
        )
        for group in range(groups)
    ]
    turns = [range(at, at + each) for at in range(0, groups, each)]

    def fetch(turn):
        for copies in (keys, values):
            for group in turns[turn]:
                copies[group].start()

    fetch(0)
    for turn, members in enumerate(turns):
        if turn + 1 < len(turns):
            fetch(turn + 1)
        factors = []
        for group in members:
            keys[group].wait()
            if turn > 0:
                values[group].wait()
        for group in members:
            factors.append(inverse_norm(k_buf[group]))
        for group, factor in zip(members, factors):
            kt_buf[group] = scaled(k_buf[group], factor).T
        if turn == 0:
            for group in members:
                values[group].wait()
        for group in members:
            for pair in range(WIDE // LANES):
                cut = slice(pair * LANES, (pair + 1) * LANES)
                held[group * (WIDE // LANES) + pair] = pair_state(
                    kt_buf[group, cut, :], v_buf[group, :, cut]
                )
        for group in members:
            stores[group].start()
    for index, out in enumerate(outs):
        first = (where_ref[0] ^ index) * 4
        for pair in range(4):
            out[pair] = held[first + pair]
    for copy in stores:
        copy.wait()


def device_totals(place, keys, values):
    rows, width = keys.shape
    groups = width // WIDE
    here = pl.BlockSpec(memory_space=pl.ANY)
    near = pl.BlockSpec(memory_space=pltpu.VMEM)
    return pl.pallas_call(
        totals_kernel,
        out_shape=[pltpu.HBM((width, rows), keys.dtype)]
        + [jax.ShapeDtypeStruct((4, SPAN, LANES), jnp.float32)] * 4,
        in_specs=[pl.BlockSpec(memory_space=pltpu.SMEM), here, here],
        out_specs=[here] + [near] * 4,
        scratch_shapes=[
            pltpu.VMEM((groups, rows, WIDE), jnp.bfloat16),
            pltpu.VMEM((groups, rows, WIDE), jnp.bfloat16),
            pltpu.VMEM((groups, WIDE, rows), jnp.bfloat16),
            pltpu.VMEM((width // LANES, SPAN, LANES), jnp.float32),
            pltpu.SemaphoreType.DMA((groups,)),
            pltpu.SemaphoreType.DMA((groups,)),
            pltpu.SemaphoreType.DMA((groups,)),
        ],
        compiler_params=pltpu.CompilerParams(vmem_limit_bytes=mib(40)),
        cost_estimate=pl.CostEstimate(
            flops=4 * rows * width * WIDE, bytes_accessed=6 * rows * width, transcendentals=0
        ),
        name="totals",
    )(place, keys, values)


def two_span_states(turned, values):
    zero = jnp.zeros((SPAN, LANES), values.dtype)
    spread = jnp.concatenate(
        [
            jnp.concatenate([values[:SPAN], zero], axis=1),
            jnp.concatenate([zero, values[SPAN:]], axis=1),
        ],
        axis=0,
    )
    both = jnp.dot(turned, spread, preferred_element_type=jnp.float32)
    lane = lax.broadcasted_iota(jnp.int32, (SPAN, LANES), 1)
    return [
        jnp.where(lane < SPAN, both[:SPAN, at : at + LANES], both[SPAN:, at : at + LANES])
        for at in (0, LANES)
    ]


def level_scale(level):
    return math.sqrt(1.0 / 2 ** max(level - 1, 0))


def blend(states, weight):
    spans = len(states)
    mix = [None] * spans
    level = states
    for bit in range(spans.bit_length() - 1):
        size = 1 << bit
        for node in range(0, len(level), 2):
            term = level[node] * weight[1 + bit]
            for c in range((node + 1) * size, (node + 2) * size):
                mix[c] = term if mix[c] is None else mix[c] + term
        level = [level[n] + level[n + 1] for n in range(0, len(level), 2)]
    return mix


def inside_kernel(slice_of, has_tree, where_ref, w_ref, q_ref, kt_ref, v_ref, *refs):
    y_ref, qn_ref, seen_ref = refs[-3:]
    rows = q_ref.shape[0]
    spans = rows // SPAN
    query = q_ref[...]
    query = scaled(query, inverse_norm(query))
    qn_ref[...] = query
    lane = lax.broadcasted_iota(jnp.int32, (SPAN, LANES), 1)
    low = lane < SPAN
    seen = (lane % SPAN) <= lax.broadcasted_iota(jnp.int32, (SPAN, LANES), 0)
    pairs = [slice(at, at + LANES) for at in range(0, q_ref.shape[1], LANES)]
    first = lax.broadcasted_iota(jnp.int32, (1, LANES), 1) < SPAN
    head = ((where_ref[0] ^ slice_of) * 2 + pl.program_id(0)) * 4
    weights = [
        [
            jnp.where(first, w_ref[level, head + 2 * pair], w_ref[level, head + 2 * pair + 1])
            * level_scale(level)
            for level in range(spans.bit_length())
        ]
        for pair in range(len(pairs))
    ]
    parts = [slice(c * SPAN, (c + 1) * SPAN) for c in range(spans)]
    states = []
    for pair, cut in enumerate(pairs):
        states.append([])
        for block in range(spans // 2):
            part = slice(block * 2 * SPAN, (block + 1) * 2 * SPAN)
            states[pair] += two_span_states(kt_ref[cut, part], v_ref[part, cut])
    for pair, cut in enumerate(pairs):
        factor = jnp.where(seen, weights[pair][0], 0.0)
        for block in range(spans // 2):
            turned = kt_ref[cut, block * 2 * SPAN : (block + 1) * 2 * SPAN]
            moved = jnp.concatenate([turned[:, SPAN:], turned[:, :SPAN]], axis=1)
            zero = jnp.zeros((SPAN, LANES), turned.dtype)
            for odd, (top, bottom) in enumerate(((turned, moved), (moved, turned))):
                part = parts[2 * block + odd]
                right = jnp.concatenate(
                    [jnp.where(low, top[:SPAN], zero), jnp.where(low, zero, bottom[SPAN:])], axis=0
                )
                scores = jnp.dot(qn_ref[part, cut], right, preferred_element_type=jnp.float32)
                seen_ref[part, cut] = (scores * factor).astype(jnp.bfloat16)
    mixes = [blend(states[pair], weights[pair]) for pair in range(len(pairs))]
    if has_tree:
        for pair, mix in enumerate(mixes):
            tree = refs[0][pair]
            mixes[pair] = [tree if local is None else local + tree for local in mix]
    for pair, cut in enumerate(pairs):
        for c, part in enumerate(parts):
            left = seen_ref[part, cut]
            right = by_head(v_ref[part, cut], low)
            if mixes[pair][c] is not None:
                left = jnp.concatenate([left, qn_ref[part, cut]], axis=1)
                right = jnp.concatenate(
                    [right, by_head(mixes[pair][c].astype(jnp.bfloat16), low)], axis=0
                )
            y_ref[part, cut] = jnp.dot(left, right, preferred_element_type=jnp.float32).astype(
                jnp.bfloat16
            )


def inside(place, weights, queries, keys, values, slice_of, so_far, trees=()):
    rows, width = queries.shape
    steps = width // WIDE // 4
    block = pl.BlockSpec((rows, WIDE), lambda i, s: (0, (s[0] ^ slice_of) * steps + i))
    turned = pl.BlockSpec((WIDE, rows), lambda i, s: ((s[0] ^ slice_of) * steps + i, 0))
    table = pl.BlockSpec(memory_space=pltpu.SMEM)
    tree = pl.BlockSpec((2, SPAN, LANES), lambda i, s: (i, 0, 0))
    count = len(so_far)
    return pl.pallas_call(
        functools.partial(inside_kernel, slice_of, len(trees) > 0),
        out_shape=[pltpu.HBM((rows, width), jnp.bfloat16)] * 2,
        grid_spec=pltpu.PrefetchScalarGridSpec(
            num_scalar_prefetch=1,
            grid=(steps,),
            in_specs=[table, block, turned, block]
            + [tree] * len(trees)
            + [pl.BlockSpec(memory_space=pl.ANY)] * count,
            out_specs=[block, block],
            scratch_shapes=[pltpu.VMEM((rows, WIDE), jnp.bfloat16)],
        ),
        input_output_aliases={5 + len(trees) + n: n for n in range(count)},
        compiler_params=pltpu.CompilerParams(vmem_limit_bytes=mib(INSIDE_MIB)),
        cost_estimate=pl.CostEstimate(
            flops=16 * rows * WIDE * steps * WIDE,
            bytes_accessed=10 * rows * WIDE * steps,
            transcendentals=0,
        ),
        name="inside",
    )(place, weights, queries, keys, values, *trees, *so_far)


def finish_kernel(where_ref, y_ref, *refs):
    trees = refs[:3]
    q_hbm, w_ref, out_ref, left, total, q_buf, q_sem = refs[3:]
    step = pl.program_id(0)
    quarter = left.shape[1]

    def fetch(part):
        home = pl.multiple_of((where_ref[0] ^ part) * quarter, quarter)
        return pltpu.make_async_copy(
            q_hbm.at[:, pl.ds(home, quarter)], q_buf.at[part % 2], q_sem.at[part % 2]
        )

    @pl.when(step < 3)
    def _():
        fetch(step + 1).start()

    @pl.when((step > 0) & (step <= 3))
    def _():
        low = lax.broadcasted_iota(jnp.int32, (SPAN, LANES), 1) < SPAN
        blocks = []
        for slot in range(4):
            tree = trees[0][slot]
            for m in range(2, 4):
                tree = jnp.where(step == m, trees[m - 1][slot], tree)
            tree = by_head(tree.astype(jnp.bfloat16), low)
            zero = jnp.zeros_like(tree)
            blocks.append(jnp.concatenate([tree, zero] if slot % 2 == 0 else [zero, tree], axis=1))
        fetch(step).wait()
        for group in range(2):
            cut = slice(group * WIDE, (group + 1) * WIDE)
            mixed = y_ref[:, cut].astype(jnp.float32) + jnp.dot(
                q_buf[step % 2, :, cut],
                jnp.concatenate(blocks[2 * group : 2 * group + 2], axis=0),
                preferred_element_type=jnp.float32,
            )
            left[:, cut] = mixed.astype(jnp.bfloat16)

    def product(rows, cut):
        return jnp.dot(rows[...], w_ref[:, cut], preferred_element_type=jnp.float32)

    @pl.when(step == 0)
    def _():
        for n in range(total.shape[0]):
            total[n] = product(y_ref, slice(n * WIDE, (n + 1) * WIDE))

    @pl.when((step > 0) & (step < 3))
    def _():
        for n in range(total.shape[0]):
            total[n] += product(left, slice(n * WIDE, (n + 1) * WIDE))

    @pl.when(step >= 3)
    def _():
        each = out_ref.shape[1] // WIDE
        for k in range(each):
            n = jnp.maximum(step - 3, 0) * each + k
            cut = pl.ds(pl.multiple_of(n * WIDE, WIDE), WIDE)
            out_ref[:, k * WIDE : (k + 1) * WIDE] = (total[n] + product(left, cut)).astype(
                jnp.bfloat16
            )


def finish(place, mixed, query, trees, out_weight):
    rows = mixed.shape[0]
    width = out_weight.shape[0]
    quarter = width // 4
    first = pl.BlockSpec((rows, quarter), lambda i, s: (0, jnp.minimum(i, 3) ^ s[0]))
    tree = pl.BlockSpec((4, SPAN, LANES), lambda i, s: (0, 0, 0), pipeline_mode=pl.Buffered(1))
    return pl.pallas_call(
        finish_kernel,
        out_shape=jax.ShapeDtypeStruct((rows, width), jnp.bfloat16),
        grid_spec=pltpu.PrefetchScalarGridSpec(
            num_scalar_prefetch=1,
            grid=(3 + LAST,),
            in_specs=[first]
            + [tree] * 3
            + [pl.BlockSpec(memory_space=pl.ANY)]
            + [pl.BlockSpec((quarter, width), lambda i, s: (jnp.minimum(i, 3) ^ s[0], 0))],
            out_specs=pl.BlockSpec((rows, width // LAST), lambda i, s: (0, jnp.maximum(i - 3, 0))),
            scratch_shapes=[
                pltpu.VMEM((rows, quarter), jnp.bfloat16),
                pltpu.VMEM((width // WIDE, rows, WIDE), jnp.float32),
                pltpu.VMEM((2, rows, quarter), jnp.bfloat16),
                pltpu.SemaphoreType.DMA((2,)),
            ],
        ),
        compiler_params=pltpu.CompilerParams(vmem_limit_bytes=mib(FINISH_MIB)),
        cost_estimate=pl.CostEstimate(
            flops=2 * rows * width * (width + WIDE),
            bytes_accessed=6 * rows * width + 2 * width * width,
            transcendentals=0,
        ),
        name="finish",
    )(place, mixed, *trees, query, out_weight)


def swap(block, axis, mask):
    return lax.ppermute(block, axis, [(i, i ^ mask) for i in range(lax.axis_size(axis))])


def swap_three(block_of, axis, unit):
    arrived = []
    for m in (1, 2, 3):
        arrived.append(swap(block_of(m), axis, m * unit))
    return arrived


def picked(flag, block):
    return jnp.where(flag, block, 0.0)


def per_device(queries, keys, values, level_weights, out_weight):
    levels, _ = level_weights.shape
    inner = lax.axis_index("inner")
    outer = lax.axis_index("outer")
    x, y, core, z = inner & 3, inner >> 2, outer & 1, outer >> 1
    near_heads = lax.dynamic_slice_in_dim(level_weights, 8 * x, 8, 1).reshape(levels, 4, 2, 1)
    ours = jnp.broadcast_to(near_heads, (levels, 4, 2, SPAN)).reshape(levels, 4, 1, LANES)
    ours = [ours[level] * level_scale(level) for level in range(levels)]
    place = x.astype(jnp.int32).reshape(1)

    queries, keys, values, out_weight = map(in_hbm, (queries, keys, values, out_weight))
    turned_keys, *sent = device_totals(place, keys, values)
    turned_keys = in_hbm(turned_keys)

    def beside(arrived, done, slice_of, tree=()):
        done = inside(place, level_weights, queries, turned_keys, values, slice_of, done, tree)
        arrived, done = lax.optimization_barrier((arrived, done))
        return arrived, [in_hbm(t) for t in done]

    from_x = swap_three(lambda m: sent[m], "inner", 1)
    from_x, done = beside(from_x, (), 1)
    from_x = [sent[0]] + from_x
    group = from_x[0] + from_x[1] + from_x[2] + from_x[3]

    from_y = swap_three(lambda n: group, "inner", 4)
    from_y, done = beside(from_y, done, 2)
    from_y = [group] + from_y
    block = from_y[0] + from_y[1] + from_y[2] + from_y[3]

    other = swap(block, "outer", 1)
    both = block + other

    from_z = swap_three(lambda n: both, "outer", 2)
    from_z, done = beside(from_z, done, 3)

    upper = picked(y & 1 == 1, ours[7] * from_y[1])
    upper = upper + picked(y >> 1 == 1, ours[8] * (from_y[2] + from_y[3]))
    upper = upper + picked(core == 1, ours[9] * other)
    upper = upper + picked(z & 1 == 1, ours[10] * from_z[0])
    upper = upper + picked(z >> 1 == 1, ours[11] * (from_z[1] + from_z[2]))
    to_x = []
    for m in range(4):
        near = picked((x ^ m) & 1 == 1, ours[5] * from_x[m ^ 1])
        far = picked((x ^ m) >> 1 == 1, ours[6] * (from_x[m ^ 2] + from_x[m ^ 3]))
        to_x.append(near + far + upper)
    trees = swap_three(lambda m: to_x[m], "inner", 1)
    trees, done = beside(trees, done, 0, (to_x[0],))
    return finish(place, *done, trees, out_weight)


def solution(mesh):
    in_specs = (
        P(("outer", "inner"), None),
        P(("outer", "inner"), None),
        P(("outer", "inner"), None),
        P(),
        P(),
    )
    out_specs = P(("outer", "inner"), None)
    return jax.shard_map(per_device, mesh=mesh, in_specs=in_specs, out_specs=out_specs, check_vma=False)
```

profile of v0, /device:TPU:1, one launch (start us, length us, event | category | flops | bytes accessed | tf_op | source)
XLA Modules:
  0.0 74.1 jit_solution(11108156229604385793)
XLA Ops:
  0.0 7.0 %totals.1 = (bf16[2048,1024]{1,0:T(8,128)(2,1)}, f32[4,64,128]{2,1,0:T(8,128)S(1)}, f32[4,64,128]{2,1,0:T(8,128)S(1)}, f32[4,64,128]{2,1,0:T(8,128)S(1)}, f32[4,64,128]{2,1,0:T(8,128)S(1)}) custom-call(s32[1]{0:T(128)} %bitcast.where_ref, bf16[1024,2048]{1,0:T(8,128)(2,1)} %k_hbm.1, bf16[1024,2048]{1,0:T(8,128)(2,1)} %v_ref.7), custom_call_target="tpu_custom_call" | custom-call | flops 2147483648 | bytes 12582912 | tf_op jit(solution)/shard_map/totals/pallas_call | solution.py:121
  7.1 2.1 %collective-permute-start = (f32[4,64,128]{2,1,0:T(8,128)S(1)}, f32[4,64,128]{2,1,0:T(8,128)S(1)}, u32[]{:S(2)}, u32[]{:S(2)}) collective-permute-start(f32[4,64,128]{2,1,0:T(8,128)S(1)} %get-tuple-element.39), channel_id=1, source_target_pairs={{0,1},{1,0},{2,3},{3,2},{4,5},{5,4},{6,7},{7,6},{8,9},{9,8},{10,11... | collective-permute-start | bytes 393224 | tf_op jit(solution)/shard_map/ppermute | solution.py:366
  9.2 2.4 %collective-permute-start.1 = (f32[4,64,128]{2,1,0:T(8,128)S(1)}, f32[4,64,128]{2,1,0:T(8,128)S(1)}, u32[]{:S(2)}, u32[]{:S(2)}) collective-permute-start(f32[4,64,128]{2,1,0:T(8,128)S(1)} %get-tuple-element.40), channel_id=1, source_target_pairs={{0,2},{1,3},{2,0},{3,1},{4,6},{5,7},{6,4},{7,5},{8,10},{9,11},{10,... | collective-permute-start | bytes 393224 | tf_op jit(solution)/shard_map/ppermute | solution.py:366
  11.6 0.0 collective-permute-start.2
  11.7 4.7 %inside.4 = (bf16[1024,2048]{1,0:T(8,128)(2,1)}, bf16[1024,2048]{1,0:T(8,128)(2,1)}) custom-call(s32[1]{0:T(128)} %bitcast.where_ref, f32[12,32]{1,0:T(8,128)S(1)} %copy-done, bf16[1024,2048]{1,0:T(8,128)(2,1)} %q_ref.7, bf16[2048,1024]{1,0:T(8,128)(2,1)} %get-tuple-element.42.kt_ref, bf16[1024,2048]{1,0:T(8,128)(2,1)} %v_ref.7), custom_call_target="tpu_custom_call" | custom-call | flops 2147483648 | bytes 5242880 | tf_op jit(solution)/shard_map/inside/pallas_call | solution.py:247
  16.3 1.0 %collective-permute-done.1 = f32[4,64,128]{2,1,0:T(8,128)S(1)} collective-permute-done((f32[4,64,128]{2,1,0:T(8,128)S(1)}, f32[4,64,128]{2,1,0:T(8,128)S(1)}, u32[]{:S(2)}, u32[]{:S(2)}) %collective-permute-start.1) | collective-permute-done | bytes 131104 | tf_op jit(solution)/shard_map/ppermute | solution.py:366
  17.3 2.6 %collective-permute-done.2 = f32[4,64,128]{2,1,0:T(8,128)S(1)} collective-permute-done((f32[4,64,128]{2,1,0:T(8,128)S(1)}, f32[4,64,128]{2,1,0:T(8,128)S(1)}, u32[]{:S(2)}, u32[]{:S(2)}) %collective-permute-start.2) | collective-permute-done | bytes 131104 | tf_op jit(solution)/shard_map/ppermute | solution.py:366
  20.0 1.4 %collective-permute-start.3 = (f32[4,64,128]{2,1,0:T(8,128)S(1)}, f32[4,64,128]{2,1,0:T(8,128)S(1)}, u32[]{:S(2)}, u32[]{:S(2)}) collective-permute-start(f32[4,64,128]{2,1,0:T(8,128)S(1)} %add_add_fusion.4), channel_id=1, source_target_pairs={{0,4},{1,5},{2,6},{3,7},{4,0},{5,1},{6,2},{7,3},{8,12},{9,13},{10,... | collective-permute-start | bytes 393224 | tf_op jit(solution)/shard_map/ppermute | solution.py:366
  21.3 2.6 %collective-permute-start.4 = (f32[4,64,128]{2,1,0:T(8,128)S(1)}, f32[4,64,128]{2,1,0:T(8,128)S(1)}, u32[]{:S(2)}, u32[]{:S(2)}) collective-permute-start(f32[4,64,128]{2,1,0:T(8,128)S(1)} %add_add_fusion.4), channel_id=1, source_target_pairs={{0,8},{1,9},{2,10},{3,11},{4,12},{5,13},{6,14},{7,15},{8,0},{9,1},... | collective-permute-start | bytes 393224 | tf_op jit(solution)/shard_map/ppermute | solution.py:366
  24.0 4.6 %inside.5 = (bf16[1024,2048]{1,0:T(8,128)(2,1)}, bf16[1024,2048]{1,0:T(8,128)(2,1)}) custom-call(s32[1]{0:T(128)} %bitcast.where_ref, f32[12,32]{1,0:T(8,128)S(1)} %copy-done, bf16[1024,2048]{1,0:T(8,128)(2,1)} %q_ref.7, bf16[2048,1024]{1,0:T(8,128)(2,1)} %get-tuple-element.42.kt_ref, ...), custom_call_target="tpu_custom_call", output_to_operand_aliasing={{0}: (5, {}), {1}: (6, {})} | custom-call | flops 2147483648 | bytes 5242880 | tf_op jit(solution)/shard_map/inside/pallas_call | solution.py:247
  28.6 0.3 collective-permute-done.4
  28.9 2.9 %collective-permute-done.5 = f32[4,64,128]{2,1,0:T(8,128)S(1)} collective-permute-done((f32[4,64,128]{2,1,0:T(8,128)S(1)}, f32[4,64,128]{2,1,0:T(8,128)S(1)}, u32[]{:S(2)}, u32[]{:S(2)}) %collective-permute-start.5) | collective-permute-done | bytes 131104 | tf_op jit(solution)/shard_map/ppermute | solution.py:366
  31.9 1.4 %collective-permute-start.6 = (f32[4,64,128]{2,1,0:T(8,128)S(1)}, f32[4,64,128]{2,1,0:T(8,128)S(1)}, u32[]{:S(2)}, u32[]{:S(2)}) collective-permute-start(f32[4,64,128]{2,1,0:T(8,128)S(1)} %add_add_fusion.3), channel_id=1, source_target_pairs={{0,16},{16,0},{32,48},{48,32},{64,80},{80,64},{96,112},{112,96},{1... | collective-permute-start | bytes 393224 | tf_op jit(solution)/shard_map/ppermute | solution.py:366
  33.3 0.1 fusion.5
  33.4 0.1 mul.216
  33.5 0.1 broadcast_in_dim.33
  33.6 0.1 mul.217
  33.6 0.1 mul.222
  33.7 0.1 broadcast_in_dim.35
  33.8 0.1 mul.223
  33.9 0.1 mul.228
  34.0 0.1 broadcast_in_dim.36
  34.0 0.1 mul.229
  34.1 0.1 mul.234
  34.2 0.1 broadcast_in_dim.37
  34.3 0.1 mul.235
  34.4 0.1 mul.240
  34.4 0.1 broadcast_in_dim.38
  34.5 0.1 mul.241
  34.6 0.1 mul.246
  34.7 0.1 broadcast_in_dim.39
  34.8 0.1 mul.247
  34.8 0.1 mul.252
  34.9 0.1 broadcast_in_dim.40
  35.0 0.1 mul.253
  35.1 1.7 %collective-permute-start.7 = (f32[4,64,128]{2,1,0:T(8,128)S(1)}, f32[4,64,128]{2,1,0:T(8,128)S(1)}, u32[]{:S(2)}, u32[]{:S(2)}) collective-permute-start(f32[4,64,128]{2,1,0:T(8,128)S(1)} %add.84), channel_id=1, source_target_pairs={{0,32},{16,48},{32,0},{48,16},{64,96},{80,112},{96,64},{112,80},{1... | collective-permute-start | bytes 393224 | tf_op jit(solution)/shard_map/ppermute | solution.py:366
  36.8 3.3 %collective-permute-start.8 = (f32[4,64,128]{2,1,0:T(8,128)S(1)}, f32[4,64,128]{2,1,0:T(8,128)S(1)}, u32[]{:S(2)}, u32[]{:S(2)}) collective-permute-start(f32[4,64,128]{2,1,0:T(8,128)S(1)} %add.84), channel_id=1, source_target_pairs={{0,64},{16,80},{32,96},{48,112},{64,0},{80,16},{96,32},{112,48},{1... | collective-permute-start | bytes 393224 | tf_op jit(solution)/shard_map/ppermute | solution.py:366
  40.1 4.6 %inside.6 = (bf16[1024,2048]{1,0:T(8,128)(2,1)}, bf16[1024,2048]{1,0:T(8,128)(2,1)}) custom-call(s32[1]{0:T(128)} %bitcast.where_ref, f32[12,32]{1,0:T(8,128)S(1)} %copy-done, bf16[1024,2048]{1,0:T(8,128)(2,1)} %q_ref.7, bf16[2048,1024]{1,0:T(8,128)(2,1)} %get-tuple-element.42.kt_ref, ...), custom_call_target="tpu_custom_call", output_to_operand_aliasing={{0}: (5, {}), {1}: (6, {})} | custom-call | flops 2147483648 | bytes 5242880 | tf_op jit(solution)/shard_map/inside/pallas_call | solution.py:247
  44.8 1.8 %collective-permute-done.8 = f32[4,64,128]{2,1,0:T(8,128)S(1)} collective-permute-done((f32[4,64,128]{2,1,0:T(8,128)S(1)}, f32[4,64,128]{2,1,0:T(8,128)S(1)}, u32[]{:S(2)}, u32[]{:S(2)}) %collective-permute-start.8) | collective-permute-done | bytes 131104 | tf_op jit(solution)/shard_map/ppermute | solution.py:366
  46.5 2.5 %collective-permute-done.9 = f32[4,64,128]{2,1,0:T(8,128)S(1)} collective-permute-done((f32[4,64,128]{2,1,0:T(8,128)S(1)}, f32[4,64,128]{2,1,0:T(8,128)S(1)}, u32[]{:S(2)}, u32[]{:S(2)}) %collective-permute-start.9) | collective-permute-done | bytes 131104 | tf_op jit(solution)/shard_map/ppermute | solution.py:366
  49.1 0.2 add_add_fusion
  49.2 0.1 add_add_fusion.1
  49.4 0.1 collective-permute-start.10
  49.4 2.0 %collective-permute-start.11 = (f32[4,64,128]{2,1,0:T(8,128)S(1)}, f32[4,64,128]{2,1,0:T(8,128)S(1)}, u32[]{:S(2)}, u32[]{:S(2)}) collective-permute-start(f32[4,64,128]{2,1,0:T(8,128)S(1)} %get-tuple-element.81), channel_id=1, source_target_pairs={{0,2},{1,3},{2,0},{3,1},{4,6},{5,7},{6,4},{7,5},{8,10},{9,11},{10,... | collective-permute-start | bytes 393224 | tf_op jit(solution)/shard_map/ppermute | solution.py:366
  51.4 1.9 %collective-permute-start.12 = (f32[4,64,128]{2,1,0:T(8,128)S(1)}, f32[4,64,128]{2,1,0:T(8,128)S(1)}, u32[]{:S(2)}, u32[]{:S(2)}) collective-permute-start(f32[4,64,128]{2,1,0:T(8,128)S(1)} %get-tuple-element.80), channel_id=1, source_target_pairs={{0,3},{1,2},{2,1},{3,0},{4,7},{5,6},{6,5},{7,4},{8,11},{9,10},{10,... | collective-permute-start | bytes 393224 | tf_op jit(solution)/shard_map/ppermute | solution.py:366
  53.3 4.7 %inside.7 = (bf16[1024,2048]{1,0:T(8,128)(2,1)}, bf16[1024,2048]{1,0:T(8,128)(2,1)}) custom-call(s32[1]{0:T(128)} %bitcast.where_ref, f32[12,32]{1,0:T(8,128)S(1)} %copy-done, bf16[1024,2048]{1,0:T(8,128)(2,1)} %q_ref.7, bf16[2048,1024]{1,0:T(8,128)(2,1)} %get-tuple-element.42.kt_ref, ...), custom_call_target="tpu_custom_call", output_to_operand_aliasing={{0}: (6, {}), {1}: (7, {})} | custom-call | flops 2147483648 | bytes 5242880 | tf_op jit(solution)/shard_map/inside/pallas_call | solution.py:247
  58.0 1.6 %collective-permute-done.12.refs_2_ = f32[4,64,128]{2,1,0:T(8,128)S(1)} collective-permute-done((f32[4,64,128]{2,1,0:T(8,128)S(1)}, f32[4,64,128]{2,1,0:T(8,128)S(1)}, u32[]{:S(2)}, u32[]{:S(2)}) %collective-permute-start.12) | collective-permute-done | bytes 131104 | tf_op jit(solution)/shard_map/ppermute | solution.py:366
  59.6 14.4 %finish.1 = bf16[1024,2048]{1,0:T(8,128)(2,1)} custom-call(s32[1]{0:T(128)} %bitcast.where_ref, bf16[1024,2048]{1,0:T(8,128)(2,1)} %get-tuple-element.66.y_ref, f32[4,64,128]{2,1,0:T(8,128)S(1)} %collective-permute-done.10.refs_0_, f32[4,64,128]{2,1,0:T(8,128)S(1)} %collective-permute-done.11.refs_1_, f32[4,64,128]{2,1,0:T(8,128)S(1)} %collective-permute-done.12.refs_2_, ...), custom_call_target="tpu_custom_call" | custom-call | flops 9663676416 | bytes 20971520 | tf_op jit(solution)/shard_map/finish/pallas_call | solution.py:337
  (13 shorter events, 0.1 us)
Async XLA Ops:
  0.0 11.7 %copy-start = (f32[12,32]{1,0:T(8,128)S(1)}, f32[12,32]{1,0:T(8,128)}, u32[]{:S(2)}) copy-start(f32[12,32]{1,0:T(8,128)} %w_ref.7) | copy-start | bytes 4612
  7.1 9.3 %collective-permute-start = (f32[4,64,128]{2,1,0:T(8,128)S(1)}, f32[4,64,128]{2,1,0:T(8,128)S(1)}, u32[]{:S(2)}, u32[]{:S(2)}) collective-permute-start(f32[4,64,128]{2,1,0:T(8,128)S(1)} %get-tuple-element.39), channel_id=1, source_target_pairs={{0,1},{1,0},{2,3},{3,2},{4,5},{5,4},{6,7},{7,6},{8,9},{9,8},{10,11... | collective-permute-start | bytes 393224 | tf_op jit(solution)/shard_map/ppermute | solution.py:366
  9.2 8.2 %collective-permute-start.1 = (f32[4,64,128]{2,1,0:T(8,128)S(1)}, f32[4,64,128]{2,1,0:T(8,128)S(1)}, u32[]{:S(2)}, u32[]{:S(2)}) collective-permute-start(f32[4,64,128]{2,1,0:T(8,128)S(1)} %get-tuple-element.40), channel_id=1, source_target_pairs={{0,2},{1,3},{2,0},{3,1},{4,6},{5,7},{6,4},{7,5},{8,10},{9,11},{10,... | collective-permute-start | bytes 393224 | tf_op jit(solution)/shard_map/ppermute | solution.py:366
  11.6 8.3 %collective-permute-start.2 = (f32[4,64,128]{2,1,0:T(8,128)S(1)}, f32[4,64,128]{2,1,0:T(8,128)S(1)}, u32[]{:S(2)}, u32[]{:S(2)}) collective-permute-start(f32[4,64,128]{2,1,0:T(8,128)S(1)} %get-tuple-element.41), channel_id=1, source_target_pairs={{0,3},{1,2},{2,1},{3,0},{4,7},{5,6},{6,5},{7,4},{8,11},{9,10},{10,... | collective-permute-start | bytes 393224 | tf_op jit(solution)/shard_map/ppermute | solution.py:366
  20.0 8.7 %collective-permute-start.3 = (f32[4,64,128]{2,1,0:T(8,128)S(1)}, f32[4,64,128]{2,1,0:T(8,128)S(1)}, u32[]{:S(2)}, u32[]{:S(2)}) collective-permute-start(f32[4,64,128]{2,1,0:T(8,128)S(1)} %add_add_fusion.4), channel_id=1, source_target_pairs={{0,4},{1,5},{2,6},{3,7},{4,0},{5,1},{6,2},{7,3},{8,12},{9,13},{10,... | collective-permute-start | bytes 393224 | tf_op jit(solution)/shard_map/ppermute | solution.py:366
  21.3 7.6 %collective-permute-start.4 = (f32[4,64,128]{2,1,0:T(8,128)S(1)}, f32[4,64,128]{2,1,0:T(8,128)S(1)}, u32[]{:S(2)}, u32[]{:S(2)}) collective-permute-start(f32[4,64,128]{2,1,0:T(8,128)S(1)} %add_add_fusion.4), channel_id=1, source_target_pairs={{0,8},{1,9},{2,10},{3,11},{4,12},{5,13},{6,14},{7,15},{8,0},{9,1},... | collective-permute-start | bytes 393224 | tf_op jit(solution)/shard_map/ppermute | solution.py:366
  24.0 7.9 %collective-permute-start.5 = (f32[4,64,128]{2,1,0:T(8,128)S(1)}, f32[4,64,128]{2,1,0:T(8,128)S(1)}, u32[]{:S(2)}, u32[]{:S(2)}) collective-permute-start(f32[4,64,128]{2,1,0:T(8,128)S(1)} %add_add_fusion.4), channel_id=1, source_target_pairs={{0,12},{1,13},{2,14},{3,15},{4,8},{5,9},{6,10},{7,11},{8,4},{9,5},... | collective-permute-start | bytes 393224 | tf_op jit(solution)/shard_map/ppermute | solution.py:366
  31.9 3.2 %collective-permute-start.6 = (f32[4,64,128]{2,1,0:T(8,128)S(1)}, f32[4,64,128]{2,1,0:T(8,128)S(1)}, u32[]{:S(2)}, u32[]{:S(2)}) collective-permute-start(f32[4,64,128]{2,1,0:T(8,128)S(1)} %add_add_fusion.3), channel_id=1, source_target_pairs={{0,16},{16,0},{32,48},{48,32},{64,80},{80,64},{96,112},{112,96},{1... | collective-permute-start | bytes 393224 | tf_op jit(solution)/shard_map/ppermute | solution.py:366
  35.1 9.7 %collective-permute-start.7 = (f32[4,64,128]{2,1,0:T(8,128)S(1)}, f32[4,64,128]{2,1,0:T(8,128)S(1)}, u32[]{:S(2)}, u32[]{:S(2)}) collective-permute-start(f32[4,64,128]{2,1,0:T(8,128)S(1)} %add.84), channel_id=1, source_target_pairs={{0,32},{16,48},{32,0},{48,16},{64,96},{80,112},{96,64},{112,80},{1... | collective-permute-start | bytes 393224 | tf_op jit(solution)/shard_map/ppermute | solution.py:366
  36.8 9.7 %collective-permute-start.8 = (f32[4,64,128]{2,1,0:T(8,128)S(1)}, f32[4,64,128]{2,1,0:T(8,128)S(1)}, u32[]{:S(2)}, u32[]{:S(2)}) collective-permute-start(f32[4,64,128]{2,1,0:T(8,128)S(1)} %add.84), channel_id=1, source_target_pairs={{0,64},{16,80},{32,96},{48,112},{64,0},{80,16},{96,32},{112,48},{1... | collective-permute-start | bytes 393224 | tf_op jit(solution)/shard_map/ppermute | solution.py:366
  40.1 8.9 %collective-permute-start.9 = (f32[4,64,128]{2,1,0:T(8,128)S(1)}, f32[4,64,128]{2,1,0:T(8,128)S(1)}, u32[]{:S(2)}, u32[]{:S(2)}) collective-permute-start(f32[4,64,128]{2,1,0:T(8,128)S(1)} %add.84), channel_id=1, source_target_pairs={{0,96},{16,112},{32,64},{48,80},{64,32},{80,48},{96,0},{112,16},{1... | collective-permute-start | bytes 393224 | tf_op jit(solution)/shard_map/ppermute | solution.py:366
  49.4 8.6 %collective-permute-start.10 = (f32[4,64,128]{2,1,0:T(8,128)S(1)}, f32[4,64,128]{2,1,0:T(8,128)S(1)}, u32[]{:S(2)}, u32[]{:S(2)}) collective-permute-start(f32[4,64,128]{2,1,0:T(8,128)S(1)} %get-tuple-element.82), channel_id=1, source_target_pairs={{0,1},{1,0},{2,3},{3,2},{4,5},{5,4},{6,7},{7,6},{8,9},{9,8},{10,11... | collective-permute-start | bytes 393224 | tf_op jit(solution)/shard_map/ppermute | solution.py:366
  49.4 8.6 %collective-permute-start.11 = (f32[4,64,128]{2,1,0:T(8,128)S(1)}, f32[4,64,128]{2,1,0:T(8,128)S(1)}, u32[]{:S(2)}, u32[]{:S(2)}) collective-permute-start(f32[4,64,128]{2,1,0:T(8,128)S(1)} %get-tuple-element.81), channel_id=1, source_target_pairs={{0,2},{1,3},{2,0},{3,1},{4,6},{5,7},{6,4},{7,5},{8,10},{9,11},{10,... | collective-permute-start | bytes 393224 | tf_op jit(solution)/shard_map/ppermute | solution.py:366
  51.4 8.2 %collective-permute-start.12 = (f32[4,64,128]{2,1,0:T(8,128)S(1)}, f32[4,64,128]{2,1,0:T(8,128)S(1)}, u32[]{:S(2)}, u32[]{:S(2)}) collective-permute-start(f32[4,64,128]{2,1,0:T(8,128)S(1)} %get-tuple-element.80), channel_id=1, source_target_pairs={{0,3},{1,2},{2,1},{3,0},{4,7},{5,6},{6,5},{7,4},{8,11},{9,10},{10,... | collective-permute-start | bytes 393224 | tf_op jit(solution)/shard_map/ppermute | solution.py:366
where the time goes:
time: 74.3 us; the launch traced here: 74.1 us
  Pallas kernels  40.1 us (54%)
  starting transfers between devices  19 us (26%)
  waiting for transfers between devices  12.7 us (17%)
  local copies, waits for them, and re-layouts  1.68 us (2%)
    ppermute x13, starting transfers between devices, swap(): lax.ppermute(block, axis, [(i, i ^ mask) for i in range(lax.axis_size(axi...  19 us
    pallas_call x4, Pallas kernels, inside(): pl.pallas_call(functools.partial(inside_kernel, slice_of, len(trees) > 0)...  18.6 us
    pallas_call x1, Pallas kernels, finish(): pl.pallas_call(finish_kernel, out_shape=jax.ShapeDtypeStruct((rows, width...  14.4 us
    ppermute x13, waiting for transfers between devices, swap(): lax.ppermute(block, axis, [(i, i ^ mask) for i in range(lax.axis_size(axi...  12.7 us
    pallas_call x1, Pallas kernels, device_totals(): pl.pallas_call(totals_kernel, out_shape=[pltpu.HBM((width, rows), keys.dt...  7.04 us
  transfers between devices with their start and end apart: 13, of which 7 were waited for; matrix products, arithmetic and copies ran while one was open for 2% of the time, Pallas kernels for 25%

commit v1 on v0

--- a/solution.py
+++ b/solution.py
@@ -12,7 +12,7 @@
 SPAN = 64
 LANES = 128
 WIDE = 256
-TOTALS_WIDE = 512
+TURNS = (2, 3, 3)
 LAST = 2
 INSIDE_MIB = 32
 FINISH_MIB = 40
@@ -59,7 +59,6 @@
     outs = refs[:4]
     k_buf, v_buf, kt_buf, held, k_sem, v_sem, kt_sem = refs[4:]
     groups = k_buf.shape[0]
-    each = TOTALS_WIDE // WIDE
 
     def load(hbm, buf, sem, group):
         return pltpu.make_async_copy(
@@ -74,7 +73,7 @@
         )
         for group in range(groups)
     ]
-    turns = [range(at, at + each) for at in range(0, groups, each)]
+    turns = [range(sum(TURNS[:n]), sum(TURNS[: n + 1])) for n in range(len(TURNS))]
 
     def fetch(turn):
         for copies in (keys, values):

time: 74.3 us -> 73.9 us (level)
  no operation moved by 1% of the time
where the time goes in v1:
time: 73.9 us; the launch traced here: 73.8 us
  Pallas kernels  39.7 us (54%)
  starting transfers between devices  19 us (26%)
  waiting for transfers between devices  12.7 us (17%)
  local copies, waits for them, and re-layouts  1.68 us (2%)
    ppermute x13, starting transfers between devices, swap(): lax.ppermute(block, axis, [(i, i ^ mask) for i in range(lax.axis_size(axi...  19 us
    pallas_call x4, Pallas kernels, inside(): pl.pallas_call(functools.partial(inside_kernel, slice_of, len(trees) > 0)...  18.6 us
    pallas_call x1, Pallas kernels, finish(): pl.pallas_call(finish_kernel, out_shape=jax.ShapeDtypeStruct((rows, width...  14.4 us
    ppermute x13, waiting for transfers between devices, swap(): lax.ppermute(block, axis, [(i, i ^ mask) for i in range(lax.axis_size(axi...  12.7 us
    pallas_call x1, Pallas kernels, device_totals(): pl.pallas_call(totals_kernel, out_shape=[pltpu.HBM((width, rows), keys.dt...  6.69 us
  transfers between devices with their start and end apart: 13, of which 7 were waited for; matrix products, arithmetic and copies ran while one was open for 2% of the time, Pallas kernels for 25%

profile of v1, /device:TPU:1, one launch (start us, length us, event | category | flops | bytes accessed | tf_op | source)
XLA Modules:
  0.0 73.8 jit_solution(6453326170099650266)
XLA Ops:
  0.0 6.7 %totals.1 = (bf16[2048,1024]{1,0:T(8,128)(2,1)}, f32[4,64,128]{2,1,0:T(8,128)S(1)}, f32[4,64,128]{2,1,0:T(8,128)S(1)}, f32[4,64,128]{2,1,0:T(8,128)S(1)}, f32[4,64,128]{2,1,0:T(8,128)S(1)}) custom-call(s32[1]{0:T(128)} %bitcast.where_ref, bf16[1024,2048]{1,0:T(8,128)(2,1)} %k_hbm.1, bf16[1024,2048]{1,0:T(8,128)(2,1)} %v_ref.7), custom_call_target="tpu_custom_call" | custom-call | flops 2147483648 | bytes 12582912 | tf_op jit(solution)/shard_map/totals/pallas_call | solution.py:120
  6.7 2.1 %collective-permute-start = (f32[4,64,128]{2,1,0:T(8,128)S(1)}, f32[4,64,128]{2,1,0:T(8,128)S(1)}, u32[]{:S(2)}, u32[]{:S(2)}) collective-permute-start(f32[4,64,128]{2,1,0:T(8,128)S(1)} %get-tuple-element.39), channel_id=1, source_target_pairs={{0,1},{1,0},{2,3},{3,2},{4,5},{5,4},{6,7},{7,6},{8,9},{9,8},{10,11... | collective-permute-start | bytes 393224 | tf_op jit(solution)/shard_map/ppermute | solution.py:365
  8.8 2.4 %collective-permute-start.1 = (f32[4,64,128]{2,1,0:T(8,128)S(1)}, f32[4,64,128]{2,1,0:T(8,128)S(1)}, u32[]{:S(2)}, u32[]{:S(2)}) collective-permute-start(f32[4,64,128]{2,1,0:T(8,128)S(1)} %get-tuple-element.40), channel_id=1, source_target_pairs={{0,2},{1,3},{2,0},{3,1},{4,6},{5,7},{6,4},{7,5},{8,10},{9,11},{10,... | collective-permute-start | bytes 393224 | tf_op jit(solution)/shard_map/ppermute | solution.py:365
  11.3 0.0 collective-permute-start.2
  11.3 4.7 %inside.4 = (bf16[1024,2048]{1,0:T(8,128)(2,1)}, bf16[1024,2048]{1,0:T(8,128)(2,1)}) custom-call(s32[1]{0:T(128)} %bitcast.where_ref, f32[12,32]{1,0:T(8,128)S(1)} %copy-done, bf16[1024,2048]{1,0:T(8,128)(2,1)} %q_ref.7, bf16[2048,1024]{1,0:T(8,128)(2,1)} %get-tuple-element.42.kt_ref, bf16[1024,2048]{1,0:T(8,128)(2,1)} %v_ref.7), custom_call_target="tpu_custom_call" | custom-call | flops 2147483648 | bytes 5242880 | tf_op jit(solution)/shard_map/inside/pallas_call | solution.py:246
  16.0 1.0 %collective-permute-done.1 = f32[4,64,128]{2,1,0:T(8,128)S(1)} collective-permute-done((f32[4,64,128]{2,1,0:T(8,128)S(1)}, f32[4,64,128]{2,1,0:T(8,128)S(1)}, u32[]{:S(2)}, u32[]{:S(2)}) %collective-permute-start.1) | collective-permute-done | bytes 131104 | tf_op jit(solution)/shard_map/ppermute | solution.py:365
  17.0 2.6 %collective-permute-done.2 = f32[4,64,128]{2,1,0:T(8,128)S(1)} collective-permute-done((f32[4,64,128]{2,1,0:T(8,128)S(1)}, f32[4,64,128]{2,1,0:T(8,128)S(1)}, u32[]{:S(2)}, u32[]{:S(2)}) %collective-permute-start.2) | collective-permute-done | bytes 131104 | tf_op jit(solution)/shard_map/ppermute | solution.py:365
  19.6 1.4 %collective-permute-start.3 = (f32[4,64,128]{2,1,0:T(8,128)S(1)}, f32[4,64,128]{2,1,0:T(8,128)S(1)}, u32[]{:S(2)}, u32[]{:S(2)}) collective-permute-start(f32[4,64,128]{2,1,0:T(8,128)S(1)} %add_add_fusion.4), channel_id=1, source_target_pairs={{0,4},{1,5},{2,6},{3,7},{4,0},{5,1},{6,2},{7,3},{8,12},{9,13},{10,... | collective-permute-start | bytes 393224 | tf_op jit(solution)/shard_map/ppermute | solution.py:365
  21.0 2.6 %collective-permute-start.4 = (f32[4,64,128]{2,1,0:T(8,128)S(1)}, f32[4,64,128]{2,1,0:T(8,128)S(1)}, u32[]{:S(2)}, u32[]{:S(2)}) collective-permute-start(f32[4,64,128]{2,1,0:T(8,128)S(1)} %add_add_fusion.4), channel_id=1, source_target_pairs={{0,8},{1,9},{2,10},{3,11},{4,12},{5,13},{6,14},{7,15},{8,0},{9,1},... | collective-permute-start | bytes 393224 | tf_op jit(solution)/shard_map/ppermute | solution.py:365
  23.6 4.6 %inside.5 = (bf16[1024,2048]{1,0:T(8,128)(2,1)}, bf16[1024,2048]{1,0:T(8,128)(2,1)}) custom-call(s32[1]{0:T(128)} %bitcast.where_ref, f32[12,32]{1,0:T(8,128)S(1)} %copy-done, bf16[1024,2048]{1,0:T(8,128)(2,1)} %q_ref.7, bf16[2048,1024]{1,0:T(8,128)(2,1)} %get-tuple-element.42.kt_ref, ...), custom_call_target="tpu_custom_call", output_to_operand_aliasing={{0}: (5, {}), {1}: (6, {})} | custom-call | flops 2147483648 | bytes 5242880 | tf_op jit(solution)/shard_map/inside/pallas_call | solution.py:246
  28.3 0.3 collective-permute-done.4
  28.6 2.9 %collective-permute-done.5 = f32[4,64,128]{2,1,0:T(8,128)S(1)} collective-permute-done((f32[4,64,128]{2,1,0:T(8,128)S(1)}, f32[4,64,128]{2,1,0:T(8,128)S(1)}, u32[]{:S(2)}, u32[]{:S(2)}) %collective-permute-start.5) | collective-permute-done | bytes 131104 | tf_op jit(solution)/shard_map/ppermute | solution.py:365
  31.5 1.4 %collective-permute-start.6 = (f32[4,64,128]{2,1,0:T(8,128)S(1)}, f32[4,64,128]{2,1,0:T(8,128)S(1)}, u32[]{:S(2)}, u32[]{:S(2)}) collective-permute-start(f32[4,64,128]{2,1,0:T(8,128)S(1)} %add_add_fusion.3), channel_id=1, source_target_pairs={{0,16},{16,0},{32,48},{48,32},{64,80},{80,64},{96,112},{112,96},{1... | collective-permute-start | bytes 393224 | tf_op jit(solution)/shard_map/ppermute | solution.py:365
  32.9 0.1 fusion.5
  33.0 0.1 mul.216
  33.1 0.1 broadcast_in_dim.33
  33.2 0.1 mul.217
  33.3 0.1 mul.222
  33.4 0.1 broadcast_in_dim.35
  33.4 0.1 mul.223
  33.5 0.1 mul.228
  33.6 0.1 broadcast_in_dim.36
  33.7 0.1 mul.229
  33.8 0.1 mul.234
  33.8 0.1 broadcast_in_dim.37
  33.9 0.1 mul.235
  34.0 0.1 mul.240
  34.1 0.1 broadcast_in_dim.38
  34.2 0.1 mul.241
  34.2 0.1 mul.246
  34.3 0.1 broadcast_in_dim.39
  34.4 0.1 mul.247
  34.5 0.1 mul.252
  34.6 0.1 broadcast_in_dim.40
  34.6 0.1 mul.253
  34.8 1.7 %collective-permute-start.7 = (f32[4,64,128]{2,1,0:T(8,128)S(1)}, f32[4,64,128]{2,1,0:T(8,128)S(1)}, u32[]{:S(2)}, u32[]{:S(2)}) collective-permute-start(f32[4,64,128]{2,1,0:T(8,128)S(1)} %add.84), channel_id=1, source_target_pairs={{0,32},{16,48},{32,0},{48,16},{64,96},{80,112},{96,64},{112,80},{1... | collective-permute-start | bytes 393224 | tf_op jit(solution)/shard_map/ppermute | solution.py:365
  36.5 3.3 %collective-permute-start.8 = (f32[4,64,128]{2,1,0:T(8,128)S(1)}, f32[4,64,128]{2,1,0:T(8,128)S(1)}, u32[]{:S(2)}, u32[]{:S(2)}) collective-permute-start(f32[4,64,128]{2,1,0:T(8,128)S(1)} %add.84), channel_id=1, source_target_pairs={{0,64},{16,80},{32,96},{48,112},{64,0},{80,16},{96,32},{112,48},{1... | collective-permute-start | bytes 393224 | tf_op jit(solution)/shard_map/ppermute | solution.py:365
  39.8 4.6 %inside.6 = (bf16[1024,2048]{1,0:T(8,128)(2,1)}, bf16[1024,2048]{1,0:T(8,128)(2,1)}) custom-call(s32[1]{0:T(128)} %bitcast.where_ref, f32[12,32]{1,0:T(8,128)S(1)} %copy-done, bf16[1024,2048]{1,0:T(8,128)(2,1)} %q_ref.7, bf16[2048,1024]{1,0:T(8,128)(2,1)} %get-tuple-element.42.kt_ref, ...), custom_call_target="tpu_custom_call", output_to_operand_aliasing={{0}: (5, {}), {1}: (6, {})} | custom-call | flops 2147483648 | bytes 5242880 | tf_op jit(solution)/shard_map/inside/pallas_call | solution.py:246
  44.4 1.7 %collective-permute-done.8 = f32[4,64,128]{2,1,0:T(8,128)S(1)} collective-permute-done((f32[4,64,128]{2,1,0:T(8,128)S(1)}, f32[4,64,128]{2,1,0:T(8,128)S(1)}, u32[]{:S(2)}, u32[]{:S(2)}) %collective-permute-start.8) | collective-permute-done | bytes 131104 | tf_op jit(solution)/shard_map/ppermute | solution.py:365
  46.2 2.5 %collective-permute-done.9 = f32[4,64,128]{2,1,0:T(8,128)S(1)} collective-permute-done((f32[4,64,128]{2,1,0:T(8,128)S(1)}, f32[4,64,128]{2,1,0:T(8,128)S(1)}, u32[]{:S(2)}, u32[]{:S(2)}) %collective-permute-start.9) | collective-permute-done | bytes 131104 | tf_op jit(solution)/shard_map/ppermute | solution.py:365
  48.7 0.2 add_add_fusion
  48.9 0.1 add_add_fusion.1
  49.0 0.1 collective-permute-start.10
  49.1 2.0 %collective-permute-start.11 = (f32[4,64,128]{2,1,0:T(8,128)S(1)}, f32[4,64,128]{2,1,0:T(8,128)S(1)}, u32[]{:S(2)}, u32[]{:S(2)}) collective-permute-start(f32[4,64,128]{2,1,0:T(8,128)S(1)} %get-tuple-element.81), channel_id=1, source_target_pairs={{0,2},{1,3},{2,0},{3,1},{4,6},{5,7},{6,4},{7,5},{8,10},{9,11},{10,... | collective-permute-start | bytes 393224 | tf_op jit(solution)/shard_map/ppermute | solution.py:365
  51.0 1.9 %collective-permute-start.12 = (f32[4,64,128]{2,1,0:T(8,128)S(1)}, f32[4,64,128]{2,1,0:T(8,128)S(1)}, u32[]{:S(2)}, u32[]{:S(2)}) collective-permute-start(f32[4,64,128]{2,1,0:T(8,128)S(1)} %get-tuple-element.80), channel_id=1, source_target_pairs={{0,3},{1,2},{2,1},{3,0},{4,7},{5,6},{6,5},{7,4},{8,11},{9,10},{10,... | collective-permute-start | bytes 393224 | tf_op jit(solution)/shard_map/ppermute | solution.py:365
  52.9 4.7 %inside.7 = (bf16[1024,2048]{1,0:T(8,128)(2,1)}, bf16[1024,2048]{1,0:T(8,128)(2,1)}) custom-call(s32[1]{0:T(128)} %bitcast.where_ref, f32[12,32]{1,0:T(8,128)S(1)} %copy-done, bf16[1024,2048]{1,0:T(8,128)(2,1)} %q_ref.7, bf16[2048,1024]{1,0:T(8,128)(2,1)} %get-tuple-element.42.kt_ref, ...), custom_call_target="tpu_custom_call", output_to_operand_aliasing={{0}: (6, {}), {1}: (7, {})} | custom-call | flops 2147483648 | bytes 5242880 | tf_op jit(solution)/shard_map/inside/pallas_call | solution.py:246
  57.6 1.6 %collective-permute-done.12.refs_2_ = f32[4,64,128]{2,1,0:T(8,128)S(1)} collective-permute-done((f32[4,64,128]{2,1,0:T(8,128)S(1)}, f32[4,64,128]{2,1,0:T(8,128)S(1)}, u32[]{:S(2)}, u32[]{:S(2)}) %collective-permute-start.12) | collective-permute-done | bytes 131104 | tf_op jit(solution)/shard_map/ppermute | solution.py:365
  59.2 14.4 %finish.1 = bf16[1024,2048]{1,0:T(8,128)(2,1)} custom-call(s32[1]{0:T(128)} %bitcast.where_ref, bf16[1024,2048]{1,0:T(8,128)(2,1)} %get-tuple-element.66.y_ref, f32[4,64,128]{2,1,0:T(8,128)S(1)} %collective-permute-done.10.refs_0_, f32[4,64,128]{2,1,0:T(8,128)S(1)} %collective-permute-done.11.refs_1_, f32[4,64,128]{2,1,0:T(8,128)S(1)} %collective-permute-done.12.refs_2_, ...), custom_call_target="tpu_custom_call" | custom-call | flops 9663676416 | bytes 20971520 | tf_op jit(solution)/shard_map/finish/pallas_call | solution.py:336
  (13 shorter events, 0.1 us)
Async XLA Ops:
  0.0 11.3 %copy-start = (f32[12,32]{1,0:T(8,128)S(1)}, f32[12,32]{1,0:T(8,128)}, u32[]{:S(2)}) copy-start(f32[12,32]{1,0:T(8,128)} %w_ref.7) | copy-start | bytes 4612
  6.7 9.3 %collective-permute-start = (f32[4,64,128]{2,1,0:T(8,128)S(1)}, f32[4,64,128]{2,1,0:T(8,128)S(1)}, u32[]{:S(2)}, u32[]{:S(2)}) collective-permute-start(f32[4,64,128]{2,1,0:T(8,128)S(1)} %get-tuple-element.39), channel_id=1, source_target_pairs={{0,1},{1,0},{2,3},{3,2},{4,5},{5,4},{6,7},{7,6},{8,9},{9,8},{10,11... | collective-permute-start | bytes 393224 | tf_op jit(solution)/shard_map/ppermute | solution.py:365
  8.8 8.2 %collective-permute-start.1 = (f32[4,64,128]{2,1,0:T(8,128)S(1)}, f32[4,64,128]{2,1,0:T(8,128)S(1)}, u32[]{:S(2)}, u32[]{:S(2)}) collective-permute-start(f32[4,64,128]{2,1,0:T(8,128)S(1)} %get-tuple-element.40), channel_id=1, source_target_pairs={{0,2},{1,3},{2,0},{3,1},{4,6},{5,7},{6,4},{7,5},{8,10},{9,11},{10,... | collective-permute-start | bytes 393224 | tf_op jit(solution)/shard_map/ppermute | solution.py:365
  11.3 8.3 %collective-permute-start.2 = (f32[4,64,128]{2,1,0:T(8,128)S(1)}, f32[4,64,128]{2,1,0:T(8,128)S(1)}, u32[]{:S(2)}, u32[]{:S(2)}) collective-permute-start(f32[4,64,128]{2,1,0:T(8,128)S(1)} %get-tuple-element.41), channel_id=1, source_target_pairs={{0,3},{1,2},{2,1},{3,0},{4,7},{5,6},{6,5},{7,4},{8,11},{9,10},{10,... | collective-permute-start | bytes 393224 | tf_op jit(solution)/shard_map/ppermute | solution.py:365
  19.6 8.7 %collective-permute-start.3 = (f32[4,64,128]{2,1,0:T(8,128)S(1)}, f32[4,64,128]{2,1,0:T(8,128)S(1)}, u32[]{:S(2)}, u32[]{:S(2)}) collective-permute-start(f32[4,64,128]{2,1,0:T(8,128)S(1)} %add_add_fusion.4), channel_id=1, source_target_pairs={{0,4},{1,5},{2,6},{3,7},{4,0},{5,1},{6,2},{7,3},{8,12},{9,13},{10,... | collective-permute-start | bytes 393224 | tf_op jit(solution)/shard_map/ppermute | solution.py:365
  21.0 7.6 %collective-permute-start.4 = (f32[4,64,128]{2,1,0:T(8,128)S(1)}, f32[4,64,128]{2,1,0:T(8,128)S(1)}, u32[]{:S(2)}, u32[]{:S(2)}) collective-permute-start(f32[4,64,128]{2,1,0:T(8,128)S(1)} %add_add_fusion.4), channel_id=1, source_target_pairs={{0,8},{1,9},{2,10},{3,11},{4,12},{5,13},{6,14},{7,15},{8,0},{9,1},... | collective-permute-start | bytes 393224 | tf_op jit(solution)/shard_map/ppermute | solution.py:365
  23.6 7.9 %collective-permute-start.5 = (f32[4,64,128]{2,1,0:T(8,128)S(1)}, f32[4,64,128]{2,1,0:T(8,128)S(1)}, u32[]{:S(2)}, u32[]{:S(2)}) collective-permute-start(f32[4,64,128]{2,1,0:T(8,128)S(1)} %add_add_fusion.4), channel_id=1, source_target_pairs={{0,12},{1,13},{2,14},{3,15},{4,8},{5,9},{6,10},{7,11},{8,4},{9,5},... | collective-permute-start | bytes 393224 | tf_op jit(solution)/shard_map/ppermute | solution.py:365
  31.5 3.2 %collective-permute-start.6 = (f32[4,64,128]{2,1,0:T(8,128)S(1)}, f32[4,64,128]{2,1,0:T(8,128)S(1)}, u32[]{:S(2)}, u32[]{:S(2)}) collective-permute-start(f32[4,64,128]{2,1,0:T(8,128)S(1)} %add_add_fusion.3), channel_id=1, source_target_pairs={{0,16},{16,0},{32,48},{48,32},{64,80},{80,64},{96,112},{112,96},{1... | collective-permute-start | bytes 393224 | tf_op jit(solution)/shard_map/ppermute | solution.py:365
  34.8 9.6 %collective-permute-start.7 = (f32[4,64,128]{2,1,0:T(8,128)S(1)}, f32[4,64,128]{2,1,0:T(8,128)S(1)}, u32[]{:S(2)}, u32[]{:S(2)}) collective-permute-start(f32[4,64,128]{2,1,0:T(8,128)S(1)} %add.84), channel_id=1, source_target_pairs={{0,32},{16,48},{32,0},{48,16},{64,96},{80,112},{96,64},{112,80},{1... | collective-permute-start | bytes 393224 | tf_op jit(solution)/shard_map/ppermute | solution.py:365
  36.5 9.7 %collective-permute-start.8 = (f32[4,64,128]{2,1,0:T(8,128)S(1)}, f32[4,64,128]{2,1,0:T(8,128)S(1)}, u32[]{:S(2)}, u32[]{:S(2)}) collective-permute-start(f32[4,64,128]{2,1,0:T(8,128)S(1)} %add.84), channel_id=1, source_target_pairs={{0,64},{16,80},{32,96},{48,112},{64,0},{80,16},{96,32},{112,48},{1... | collective-permute-start | bytes 393224 | tf_op jit(solution)/shard_map/ppermute | solution.py:365
  39.8 8.9 %collective-permute-start.9 = (f32[4,64,128]{2,1,0:T(8,128)S(1)}, f32[4,64,128]{2,1,0:T(8,128)S(1)}, u32[]{:S(2)}, u32[]{:S(2)}) collective-permute-start(f32[4,64,128]{2,1,0:T(8,128)S(1)} %add.84), channel_id=1, source_target_pairs={{0,96},{16,112},{32,64},{48,80},{64,32},{80,48},{96,0},{112,16},{1... | collective-permute-start | bytes 393224 | tf_op jit(solution)/shard_map/ppermute | solution.py:365
  49.0 8.6 %collective-permute-start.10 = (f32[4,64,128]{2,1,0:T(8,128)S(1)}, f32[4,64,128]{2,1,0:T(8,128)S(1)}, u32[]{:S(2)}, u32[]{:S(2)}) collective-permute-start(f32[4,64,128]{2,1,0:T(8,128)S(1)} %get-tuple-element.82), channel_id=1, source_target_pairs={{0,1},{1,0},{2,3},{3,2},{4,5},{5,4},{6,7},{7,6},{8,9},{9,8},{10,11... | collective-permute-start | bytes 393224 | tf_op jit(solution)/shard_map/ppermute | solution.py:365
  49.1 8.6 %collective-permute-start.11 = (f32[4,64,128]{2,1,0:T(8,128)S(1)}, f32[4,64,128]{2,1,0:T(8,128)S(1)}, u32[]{:S(2)}, u32[]{:S(2)}) collective-permute-start(f32[4,64,128]{2,1,0:T(8,128)S(1)} %get-tuple-element.81), channel_id=1, source_target_pairs={{0,2},{1,3},{2,0},{3,1},{4,6},{5,7},{6,4},{7,5},{8,10},{9,11},{10,... | collective-permute-start | bytes 393224 | tf_op jit(solution)/shard_map/ppermute | solution.py:365
  51.0 8.2 %collective-permute-start.12 = (f32[4,64,128]{2,1,0:T(8,128)S(1)}, f32[4,64,128]{2,1,0:T(8,128)S(1)}, u32[]{:S(2)}, u32[]{:S(2)}) collective-permute-start(f32[4,64,128]{2,1,0:T(8,128)S(1)} %get-tuple-element.80), channel_id=1, source_target_pairs={{0,3},{1,2},{2,1},{3,0},{4,7},{5,6},{6,5},{7,4},{8,11},{9,10},{10,... | collective-permute-start | bytes 393224 | tf_op jit(solution)/shard_map/ppermute | solution.py:365
